TPU v7x, 512 devices: a whole 4x4x16 slice. The times are simulated.
512 devices in a mesh: dp: 16 (over y, z_hi, core), expert: 32 (over z_lo, x).
Axes of the slice: x: 4, y: 4, z: 16 (z_hi: 2, z_lo: 8; z = z_hi * 8 + z_lo), core: 2. Of those that a mesh axis runs over, the one named last changes fastest.
Arguments:
- tokens: bfloat16 [1536, 3584], P('dp', 'expert'), may hold values from -13 to 13
- routes: int32 [1536, 8], replicated, may hold values from 0 to 31, all different within a row; in each aligned block of 96 rows (0 to 95, 96 to 191, ...) at most 32 rows name the same one
- gate_weight: bfloat16 [32, 3584, 2048], P('expert', None, 'dp'), may hold values from -0.09375 to 0.09375
- up_weight: bfloat16 [32, 3584, 2048], P('expert', None, 'dp'), may hold values from -0.09375 to 0.09375
- hidden_grad: bfloat16 [32, 16, 32, 2048], P('expert', None, None, 'dp'), may hold values from -40 to 40
- clip_limit: float32 [32], P('expert'), may hold values from 1 to 40
Outputs:
- hidden: bfloat16 [32, 16, 32, 2048], P('expert', None, None, 'dp')
- grad_gate: bfloat16 [32, 3584, 2048], P('expert', None, 'dp')
- grad_up: bfloat16 [32, 3584, 2048], P('expert', None, 'dp')
- token_grad: bfloat16 [1536, 3584], P('dp', 'expert')
Inputs may be any that keep to these rules, and one draw needn't show every extreme that they name: `routes`: each row names 8 different experts. In each aligned block of 96 rows (the tokens of one index of dp) no expert is named by more than 32 rows, a bound that some block reaches.
All inputs are finite; a program needn't handle non-finite values.
Results may differ from a plain program's by a relative error of at most 0.014.
Values may be sent and summed in bfloat16 or wider, within the bound.
No kernel may reach another device: no remote copies, remote signals or barrier semaphores. Data moves between devices by JAX's collectives and lax.ppermute only.
A program may use at most 64 MiB of HBM per device.

v0:
```python
import jax
import jax.numpy as jnp
from jax import lax
from jax.sharding import Mesh, PartitionSpec as P


BF = jnp.bfloat16
F32 = jnp.float32


def shift(value, axis, step):
    size = lax.axis_size(axis)
    return lax.ppermute(value, axis, [(i, (i + step) % size) for i in range(size)])


def swap(value, axis, bit):
    size = lax.axis_size(axis)
    return lax.ppermute(value, axis, [(i, i ^ bit) for i in range(size)])


def pick(index, items):
    return lax.select_n(index, *items)


def slot_onehot(routes, yi, ci, zli, n_y, n_x, tok, top, cap):
    blocks = routes.reshape(n_y, 2, 2, tok, top)
    own = lax.dynamic_index_in_dim(blocks, yi, 0, keepdims=False)
    own = lax.dynamic_index_in_dim(own, ci, 1, keepdims=False)
    experts = zli * n_x + jnp.arange(n_x, dtype=jnp.int32)
    named = jnp.any(own[:, None, :, :] == experts[None, :, None, None], axis=3)
    row = lax.broadcasted_iota(jnp.int32, (tok, tok), 0)
    col = lax.broadcasted_iota(jnp.int32, (tok, tok), 1)
    earlier = (row < col).astype(BF)
    rank = lax.dot_general(
        named.astype(BF), earlier, (((2,), (0,)), ((), ())), preferred_element_type=F32
    )
    rank = jnp.where(named, rank, -1.0)
    slots = lax.broadcasted_iota(jnp.int32, (1, 1, cap, 1), 2).astype(F32)
    return (rank[:, :, None, :] == slots).astype(BF)


def body(tokens, routes, gate_weight, up_weight, hidden_grad, clip_limit):
    n_y, n_x, n_zl = lax.axis_size("y"), lax.axis_size("x"), lax.axis_size("zl")
    n_dp, n_z = n_y * 4, 2 * n_zl
    yi, ci, zli = lax.axis_index("y"), lax.axis_index("core"), lax.axis_index("zl")
    tok, feat = tokens.shape
    top = routes.shape[1]
    width, units = gate_weight.shape[1:]
    cap = hidden_grad.shape[2]
    part = n_zl * feat
    rows = 2 * cap

    along_z = lax.all_gather(tokens.T, ("zh", "zl"), axis=0, tiled=True)
    along_z = along_z.reshape(2, part, tok)

    onehot = slot_onehot(routes, yi, ci, zli, n_y, n_x, tok, top, cap)
    onehot = onehot.reshape(2, n_x * cap, tok)

    def permuted(weight):
        return weight[0].reshape(n_zl, n_x, feat, units).transpose(1, 0, 2, 3).reshape(width, units)

    weights = jnp.concatenate([permuted(gate_weight), permuted(up_weight)], axis=1)

    outgoing = lax.dot_general(
        onehot, along_z, (((2,), (2,)), ((0,), (0,))), preferred_element_type=F32
    ).astype(BF)
    outgoing = outgoing.reshape(2, n_x, cap, part).transpose(1, 0, 2, 3).reshape(n_x, rows, part)
    arrived = lax.all_to_all(outgoing, "x", 0, 0, tiled=True)
    own = jnp.concatenate([arrived[j] for j in range(n_x)], axis=1)

    a1, a3, a2 = shift(own, "y", 1), shift(own, "y", -1), shift(own, "y", 2)
    a_of = {(0,): own, (1, 3): jnp.concatenate([a1, a3], axis=0), (2,): a2}

    grads = hidden_grad[0].reshape(n_y, 2, 2, cap, units).transpose(0, 2, 1, 3, 4)

    def math(x_rows, grad_rows):
        pre = jnp.dot(x_rows, weights, preferred_element_type=F32)
        gate_pre, up_pre = pre[:, :units], pre[:, units:]
        sigma = jax.nn.sigmoid(gate_pre)
        hidden = (gate_pre * sigma * up_pre).astype(BF)
        g = grad_rows.astype(F32)
        up_act = (g * gate_pre * sigma).astype(BF)
        gate_act = (g * up_pre * sigma * (1.0 + gate_pre * (1.0 - sigma))).astype(BF)
        act = jnp.concatenate([gate_act, up_act], axis=1)
        partial = lax.dot_general(
            act, weights, (((1,), (1,)), ((), ())), preferred_element_type=F32
        )
        return hidden, act, partial

    def grad_rows_of(group):
        picked = [lax.dynamic_index_in_dim(grads, (yi - r) % n_y, 0) for r in group]
        both = jnp.concatenate(picked, axis=0).transpose(1, 0, 2, 3, 4)
        return jnp.where(ci == 0, both, both[::-1]).reshape(-1, units)

    x_list, act_list, hidden_of, summed = [], [], {}, {}
    for group in ((0,), (1, 3), (2,)):
        count = len(group) * rows
        x_rows = jnp.concatenate([a_of[group], swap(a_of[group], "core", 1)], axis=0)
        hid, act, partial = math(x_rows, grad_rows_of(group))
        x_list.append(x_rows)
        act_list.append(act)
        both = partial[:count] + swap(partial[count:].astype(BF), "core", 1).astype(F32)
        hid = hid.reshape(2, len(group), 2, cap, units)
        hid = jnp.where(ci == 0, hid, hid[::-1])
        for n, r in enumerate(group):
            hidden_of[r] = hid[:, n]
            summed[r] = both[n * rows : (n + 1) * rows]

    got = [shift(summed[r].astype(BF), "y", -r).astype(F32) for r in (1, 3, 2)]
    slot_grad = (summed[0] + got[0] + got[1] + got[2]).astype(BF)

    back = jnp.stack([slot_grad[:, j * part : (j + 1) * part] for j in range(n_x)])
    back = lax.all_to_all(back, "x", 0, 0, tiled=True)
    back = back.reshape(n_x, 2, cap, part).transpose(1, 0, 2, 3).reshape(2, n_x * cap, part)
    token_sum = lax.dot_general(
        back, onehot, (((1,), (1,)), ((0,), (0,))), preferred_element_type=F32
    ).reshape(n_z, feat, tok)

    x_all = jnp.concatenate(x_list, axis=0)
    act_all = jnp.concatenate(act_list, axis=0)
    raw = lax.dot_general(x_all, act_all, (((0,), (0,)), ((), ())), preferred_element_type=F32)
    total = jnp.sum(raw * raw).reshape(1)
    total = total + swap(total, "core", 1)
    total = total + swap(total, "y", 1)
    total = total + swap(total, "y", 2)

    sent, total = lax.optimization_barrier((token_sum.astype(BF), total))
    landed = lax.all_to_all(sent, ("zh", "zl"), 0, 0, tiled=True)
    token_grad = jnp.sum(landed.astype(F32), axis=0).astype(BF).T
    other_half = swap(total, "zh", 1)
    total = total + other_half
    root_mean = jnp.sqrt(total / (2.0 * width * units * n_dp) + 1e-06)
    clip_scale = jnp.minimum(1.0, clip_limit / root_mean)
    scaled = (clip_scale[:, None] * raw).astype(BF)

    def restored(value):
        return value.reshape(n_x, n_zl, feat, units).transpose(1, 0, 2, 3).reshape(1, width, units)

    hidden = jnp.stack(
        [pick((yi - j) % n_y, [hidden_of[r] for r in range(n_y)]) for j in range(n_y)]
    )
    hidden = hidden.transpose(0, 2, 1, 3, 4).reshape(1, n_dp, cap, units)
    return (hidden, restored(scaled[:, :units]), restored(scaled[:, units:]), token_grad)


def physical(mesh):
    experts = mesh.shape["expert"]
    devices = mesh.devices.reshape(mesh.shape["dp"] // 4, 2, 2, experts // 4, 4)
    return Mesh(devices, ("y", "zh", "core", "zl", "x"))


def solution(mesh):
    dp, expert = ("y", "zh", "core"), ("zl", "x")
    return jax.shard_map(
        body,
        mesh=physical(mesh),
        in_specs=(
            P(dp, expert),
            P(),
            P(expert, None, dp),
            P(expert, None, dp),
            P(expert, None, None, dp),
            P(expert),
        ),
        out_specs=(
            P(expert, None, None, dp),
            P(expert, None, dp),
            P(expert, None, dp),
            P(dp, expert),
        ),
        check_vma=False,
    )
```

profile of v0, /device:TPU:36, one launch (start us, length us, event | category | flops | bytes accessed | tf_op | source)
XLA Modules:
  0.0 177.6 jit_solution(6604066923780260444)
XLA Ops:
  2.1 35.6 %all-gather = bf16[16,112,96]{1,2,0:T(8,128)(2,1)S(1)} all-gather(bf16[1,112,96]{1,2,0:T(8,128)(2,1)} %bitcast.148), channel_id=1, replica_groups=mesh['y'=4,'zh'=2,'core'=2,'zl'=8,'x'=4] {'zh','zl'}, dimensions={0}, use_global_device_ids=true | all-gather | bytes 365568 | tf_op jit(solution)/shard_map/all_gather | solution.py:53
  39.9 4.8 %all-to-all-start = ((bf16[4,64,896]{2,1,0:T(8,128)(2,1)}), bf16[4,64,896]{2,1,0:T(8,128)(2,1)S(1)}, u32[]{:S(2)}, u32[]{:S(2)}) async-start(bf16[4,64,896]{2,1,0:T(8,128)(2,1)} %bitcast.7), calls=%async_computation | async-start | bytes 917504 | tf_op jit(solution)/shard_map/all_to_all | solution.py:68
  44.7 4.7 %all-to-all-done = bf16[4,64,896]{2,1,0:T(8,128)(2,1)S(1)} async-done(((bf16[4,64,896]{2,1,0:T(8,128)(2,1)}), bf16[4,64,896]{2,1,0:T(8,128)(2,1)S(1)}, u32[]{:S(2)}, u32[]{:S(2)}) %all-to-all-start) | async-done | bytes 458784 | tf_op jit(solution)/shard_map/all_to_all | solution.py:68
  50.5 3.5 %collective-permute-start.1 = (bf16[64,3584]{1,0:T(8,128)(2,1)}, bf16[64,3584]{1,0:T(8,128)(2,1)S(1)}, u32[]{:S(2)}, u32[]{:S(2)}) collective-permute-start(bf16[64,3584]{1,0:T(8,128)(2,1)} %get-tuple-element.17), channel_id=1, source_target_pairs={{0,128},{128,256},{256,384},{384,0},{1,129},{129,257},{257,385},{3... | collective-permute-start | bytes 1376264 | tf_op jit(solution)/shard_map/ppermute | solution.py:13
  53.9 3.6 %collective-permute-start.2 = (bf16[64,3584]{1,0:T(8,128)(2,1)}, bf16[64,3584]{1,0:T(8,128)(2,1)S(1)}, u32[]{:S(2)}, u32[]{:S(2)}) collective-permute-start(bf16[64,3584]{1,0:T(8,128)(2,1)} %get-tuple-element.17), channel_id=1, source_target_pairs={{0,384},{128,0},{256,128},{384,256},{1,385},{129,1},{257,129},{385... | collective-permute-start | bytes 1376264 | tf_op jit(solution)/shard_map/ppermute | solution.py:13
  58.5 1.9 %collective-permute-start = (bf16[64,3584]{1,0:T(8,128)(2,1)}, bf16[64,3584]{1,0:T(8,128)(2,1)S(1)}, u32[]{:S(2)}, u32[]{:S(2)}) collective-permute-start(bf16[64,3584]{1,0:T(8,128)(2,1)} %get-tuple-element.17), channel_id=1, source_target_pairs={{0,32},{32,0},{1,33},{33,1},{2,34},{34,2},{3,35},{35,3},{4,36},{36... | collective-permute-start | bytes 1376264 | tf_op jit(solution)/shard_map/ppermute | solution.py:18
  60.4 3.9 %collective-permute-start.4 = (bf16[64,3584]{1,0:T(8,128)(2,1)}, bf16[64,3584]{1,0:T(8,128)(2,1)S(1)}, u32[]{:S(2)}, u32[]{:S(2)}) collective-permute-start(bf16[64,3584]{1,0:T(8,128)(2,1)} %get-tuple-element.17), channel_id=1, source_target_pairs={{0,256},{128,384},{256,0},{384,128},{1,257},{129,385},{257,1},{385... | collective-permute-start | bytes 1376264 | tf_op jit(solution)/shard_map/ppermute | solution.py:13
  64.6 1.9 %collective-permute-start.3 = (bf16[128,3584]{1,0:T(8,128)(2,1)S(1)}, bf16[128,3584]{1,0:T(8,128)(2,1)S(1)}, u32[]{:S(2)}, u32[]{:S(2)}) collective-permute-start(bf16[128,3584]{1,0:T(8,128)(2,1)S(1)} %pad_maximum_fusion.1), channel_id=1, source_target_pairs={{0,32},{32,0},{1,33},{33,1},{2,34},{34,2},{3,35},{35,3},{4,36},{36... | collective-permute-start | bytes 2752520 | tf_op jit(solution)/shard_map/ppermute | solution.py:18
  67.8 2.5 %collective-permute-start.6 = (bf16[64,3584]{1,0:T(8,128)(2,1)S(1)}, bf16[64,3584]{1,0:T(8,128)(2,1)S(1)}, u32[]{:S(2)}, u32[]{:S(2)}) collective-permute-start(bf16[64,3584]{1,0:T(8,128)(2,1)S(1)} %slice.186), channel_id=1, source_target_pairs={{0,32},{32,0},{1,33},{33,1},{2,34},{34,2},{3,35},{35,3},{4,36},{36... | collective-permute-start | bytes 1376264 | tf_op jit(solution)/shard_map/ppermute | solution.py:18
  70.5 6.5 %collective-permute-done.4 = bf16[64,3584]{1,0:T(8,128)(2,1)S(1)} collective-permute-done((bf16[64,3584]{1,0:T(8,128)(2,1)}, bf16[64,3584]{1,0:T(8,128)(2,1)S(1)}, u32[]{:S(2)}, u32[]{:S(2)}) %collective-permute-start.4) | collective-permute-done | bytes 458784 | tf_op jit(solution)/shard_map/ppermute | solution.py:13
  81.9 2.0 %collective-permute-start.10 = (bf16[64,3584]{1,0:T(8,128)(2,1)S(1)}, bf16[64,3584]{1,0:T(8,128)(2,1)S(1)}, u32[]{:S(2)}, u32[]{:S(2)}) collective-permute-start(bf16[64,3584]{1,0:T(8,128)(2,1)S(1)} %slice.185), channel_id=1, source_target_pairs={{0,32},{32,0},{1,33},{33,1},{2,34},{34,2},{3,35},{35,3},{4,36},{36... | collective-permute-start | bytes 1376264 | tf_op jit(solution)/shard_map/ppermute | solution.py:18
  85.5 2.3 %collective-permute-start.7 = (bf16[128,3584]{1,0:T(8,128)(2,1)S(1)}, bf16[128,3584]{1,0:T(8,128)(2,1)S(1)}, u32[]{:S(2)}, u32[]{:S(2)}) collective-permute-start(bf16[128,3584]{1,0:T(8,128)(2,1)S(1)} %slice.184), channel_id=1, source_target_pairs={{0,32},{32,0},{1,33},{33,1},{2,34},{34,2},{3,35},{35,3},{4,36},{36... | collective-permute-start | bytes 2752520 | tf_op jit(solution)/shard_map/ppermute | solution.py:18
  87.9 3.9 %collective-permute-start.11 = (bf16[64,3584]{1,0:T(8,128)(2,1)S(1)}, bf16[64,3584]{1,0:T(8,128)(2,1)S(1)}, u32[]{:S(2)}, u32[]{:S(2)}) collective-permute-start(bf16[64,3584]{1,0:T(8,128)(2,1)S(1)} %fusion.7), channel_id=1, source_target_pairs={{0,256},{128,384},{256,0},{384,128},{1,257},{129,385},{257,1},{385... | collective-permute-start | bytes 1376264 | tf_op jit(solution)/shard_map/ppermute | solution.py:13
  92.2 3.0 %collective-permute-start.8 = (bf16[64,3584]{1,0:T(8,128)(2,1)S(1)}, bf16[64,3584]{1,0:T(8,128)(2,1)S(1)}, u32[]{:S(2)}, u32[]{:S(2)}) collective-permute-start(bf16[64,3584]{1,0:T(8,128)(2,1)S(1)} %get-tuple-element.10), channel_id=1, source_target_pairs={{0,384},{128,0},{256,128},{384,256},{1,385},{129,1},{257,129},{385... | collective-permute-start | bytes 1376264 | tf_op jit(solution)/shard_map/ppermute | solution.py:13
  95.1 2.9 %collective-permute-start.9 = (bf16[64,3584]{1,0:T(8,128)(2,1)S(1)}, bf16[64,3584]{1,0:T(8,128)(2,1)S(1)}, u32[]{:S(2)}, u32[]{:S(2)}) collective-permute-start(bf16[64,3584]{1,0:T(8,128)(2,1)S(1)} %get-tuple-element.11), channel_id=1, source_target_pairs={{0,128},{128,256},{256,384},{384,0},{1,129},{129,257},{257,385},{3... | collective-permute-start | bytes 1376264 | tf_op jit(solution)/shard_map/ppermute | solution.py:13
  98.0 3.5 %multiply_reduce_fusion = (f32[]{:T(128)}, f32[3584,256]{1,0:T(8,128)}) fusion(bf16[512,3584]{1,0:T(8,128)(2,1)S(1)} %constant_dynamic-update-slice_fusion, bf16[128,128]{1,0:T(8,128)(2,1)S(1)} %get-tuple-element.28, bf16[128,128]{1,0:T(8,128)(2,1)S(1)} %get-tuple-element.27, bf16[256,128]{1,0:T(8,128)(2,1)S(1)} %get-tuple-element.23, ...), kind=kOutput, calls=%fused_computation.1 | convolution fusion | flops 942931968 | bytes 7602180 | tf_op jit(solution)/shard_map/dot_general | solution.py:121
  104.7 8.1 %collective-permute-done.8 = bf16[64,3584]{1,0:T(8,128)(2,1)S(1)} collective-permute-done((bf16[64,3584]{1,0:T(8,128)(2,1)S(1)}, bf16[64,3584]{1,0:T(8,128)(2,1)S(1)}, u32[]{:S(2)}, u32[]{:S(2)}) %collective-permute-start.8) | collective-permute-done | bytes 458784 | tf_op jit(solution)/shard_map/ppermute | solution.py:13
  114.8 6.4 %all-to-all-start.1 = ((bf16[4,64,896]{2,1,0:T(8,128)(2,1)}), bf16[4,64,896]{2,1,0:T(8,128)(2,1)S(1)}, u32[]{:S(2)}, u32[]{:S(2)}) async-start(bf16[4,64,896]{2,1,0:T(8,128)(2,1)} %pad_maximum_fusion.3), calls=%async_computation.1 | async-start | bytes 917504 | tf_op jit(solution)/shard_map/all_to_all | solution.py:113
  123.3 3.7 %collective-permute-start.13 = (f32[1]{0:T(128)}, f32[1]{0:T(128)}, u32[]{:S(2)}, u32[]{:S(2)}) collective-permute-start(f32[1]{0:T(128)} %add.131), channel_id=1, source_target_pairs={{0,128},{128,0},{256,384},{384,256},{1,129},{129,1},{257,385},{385... | collective-permute-start | bytes 20 | tf_op jit(solution)/shard_map/ppermute | solution.py:18
  129.5 5.2 %collective-permute-start.14 = (f32[1]{0:T(128)}, f32[1]{0:T(128)}, u32[]{:S(2)}, u32[]{:S(2)}) collective-permute-start(f32[1]{0:T(128)} %add.132), channel_id=1, source_target_pairs={{0,256},{128,384},{256,0},{384,128},{1,257},{129,385},{257,1},{385... | collective-permute-start | bytes 20 | tf_op jit(solution)/shard_map/ppermute | solution.py:18
  138.3 10.0 %collective-permute-start.15 = (f32[1]{0:T(128)}, f32[1]{0:T(128)}, u32[]{:S(2)}, u32[]{:S(2)}) collective-permute-start(f32[1]{0:T(128)} %add.133), channel_id=1, source_target_pairs={{0,64},{64,0},{1,65},{65,1},{2,66},{66,2},{3,67},{67,3},{4,68},{68... | collective-permute-start | bytes 20 | tf_op jit(solution)/shard_map/ppermute | solution.py:18
  149.1 7.7 %all-to-all-start.2 = ((bf16[16,112,96]{1,2,0:T(8,128)(2,1)}), bf16[16,112,96]{1,2,0:T(8,128)(2,1)S(1)}, u32[]{:S(2)}, u32[]{:S(2)}) async-start(bf16[16,112,96]{1,2,0:T(8,128)(2,1)} %copy.123), calls=%async_computation.2 | async-start | bytes 786432 | tf_op jit(solution)/shard_map/all_to_all | solution.py:128
  157.5 2.3 %multiply_convert_fusion = bf16[3584,256]{1,0:T(8,128)(2,1)S(1)} fusion(f32[3584,256]{1,0:T(8,128)} %get-tuple-element.39, f32[]{:T(128)} %bitcast.50), kind=kLoop, calls=%fused_computation | loop fusion | flops 1835008 | bytes 5505028 | tf_op jit(solution)/shard_map/convert_element_type | solution.py:134
  162.0 14.9 %all-to-all-done.2 = bf16[16,112,96]{1,2,0:T(8,128)(2,1)S(1)} async-done(((bf16[16,112,96]{1,2,0:T(8,128)(2,1)}), bf16[16,112,96]{1,2,0:T(8,128)(2,1)S(1)}, u32[]{:S(2)}, u32[]{:S(2)}) %all-to-all-start.2) | async-done | bytes 344096 | tf_op jit(solution)/shard_map/all_to_all | solution.py:128
  (94 shorter events, 27.5 us)
Async XLA Ops:
  0.6 44.0 %copy-start.2 = (bf16[1,16,32,128]{3,2,1,0:T(8,128)(2,1)S(1)}, bf16[1,16,32,128]{3,2,1,0:T(8,128)(2,1)}, u32[]{:S(2)}) copy-start(bf16[1,16,32,128]{3,2,1,0:T(8,128)(2,1)} %param.10) | copy-start | bytes 393220
  37.7 19.9 %copy-start = (bf16[1,3584,128]{2,1,0:T(8,128)(2,1)S(1)}, bf16[1,3584,128]{2,1,0:T(8,128)(2,1)}, u32[]{:S(2)}) copy-start(bf16[1,3584,128]{2,1,0:T(8,128)(2,1)} %param.8) | copy-start | bytes 2752516
  38.7 18.9 %copy-start.1 = (bf16[1,3584,128]{2,1,0:T(8,128)(2,1)S(1)}, bf16[1,3584,128]{2,1,0:T(8,128)(2,1)}, u32[]{:S(2)}) copy-start(bf16[1,3584,128]{2,1,0:T(8,128)(2,1)} %param.9) | copy-start | bytes 2752516
  39.9 9.6 %all-to-all-start = ((bf16[4,64,896]{2,1,0:T(8,128)(2,1)}), bf16[4,64,896]{2,1,0:T(8,128)(2,1)S(1)}, u32[]{:S(2)}, u32[]{:S(2)}) async-start(bf16[4,64,896]{2,1,0:T(8,128)(2,1)} %bitcast.7), calls=%async_computation | async-start | bytes 917504 | tf_op jit(solution)/shard_map/all_to_all | solution.py:68
  50.5 13.8 %collective-permute-start.1 = (bf16[64,3584]{1,0:T(8,128)(2,1)}, bf16[64,3584]{1,0:T(8,128)(2,1)S(1)}, u32[]{:S(2)}, u32[]{:S(2)}) collective-permute-start(bf16[64,3584]{1,0:T(8,128)(2,1)} %get-tuple-element.17), channel_id=1, source_target_pairs={{0,128},{128,256},{256,384},{384,0},{1,129},{129,257},{257,385},{3... | collective-permute-start | bytes 1376264 | tf_op jit(solution)/shard_map/ppermute | solution.py:13
  53.9 10.6 %collective-permute-start.2 = (bf16[64,3584]{1,0:T(8,128)(2,1)}, bf16[64,3584]{1,0:T(8,128)(2,1)S(1)}, u32[]{:S(2)}, u32[]{:S(2)}) collective-permute-start(bf16[64,3584]{1,0:T(8,128)(2,1)} %get-tuple-element.17), channel_id=1, source_target_pairs={{0,384},{128,0},{256,128},{384,256},{1,385},{129,1},{257,129},{385... | collective-permute-start | bytes 1376264 | tf_op jit(solution)/shard_map/ppermute | solution.py:13
  58.5 8.1 %collective-permute-start = (bf16[64,3584]{1,0:T(8,128)(2,1)}, bf16[64,3584]{1,0:T(8,128)(2,1)S(1)}, u32[]{:S(2)}, u32[]{:S(2)}) collective-permute-start(bf16[64,3584]{1,0:T(8,128)(2,1)} %get-tuple-element.17), channel_id=1, source_target_pairs={{0,32},{32,0},{1,33},{33,1},{2,34},{34,2},{3,35},{35,3},{4,36},{36... | collective-permute-start | bytes 1376264 | tf_op jit(solution)/shard_map/ppermute | solution.py:18
  60.4 16.5 %collective-permute-start.4 = (bf16[64,3584]{1,0:T(8,128)(2,1)}, bf16[64,3584]{1,0:T(8,128)(2,1)S(1)}, u32[]{:S(2)}, u32[]{:S(2)}) collective-permute-start(bf16[64,3584]{1,0:T(8,128)(2,1)} %get-tuple-element.17), channel_id=1, source_target_pairs={{0,256},{128,384},{256,0},{384,128},{1,257},{129,385},{257,1},{385... | collective-permute-start | bytes 1376264 | tf_op jit(solution)/shard_map/ppermute | solution.py:13
  64.6 19.3 %collective-permute-start.3 = (bf16[128,3584]{1,0:T(8,128)(2,1)S(1)}, bf16[128,3584]{1,0:T(8,128)(2,1)S(1)}, u32[]{:S(2)}, u32[]{:S(2)}) collective-permute-start(bf16[128,3584]{1,0:T(8,128)(2,1)S(1)} %pad_maximum_fusion.1), channel_id=1, source_target_pairs={{0,32},{32,0},{1,33},{33,1},{2,34},{34,2},{3,35},{35,3},{4,36},{36... | collective-permute-start | bytes 2752520 | tf_op jit(solution)/shard_map/ppermute | solution.py:18
  67.0 3.4 %copy-start.3 = (bf16[512,3584]{1,0:T(8,128)(2,1)S(1)}, bf16[512,3584]{1,0:T(8,128)(2,1)}, u32[]{:S(2)}) copy-start(bf16[512,3584]{1,0:T(8,128)(2,1)} %get-tuple-element.16) | copy-start | bytes 11010052
  67.8 35.7 %collective-permute-start.6 = (bf16[64,3584]{1,0:T(8,128)(2,1)S(1)}, bf16[64,3584]{1,0:T(8,128)(2,1)S(1)}, u32[]{:S(2)}, u32[]{:S(2)}) collective-permute-start(bf16[64,3584]{1,0:T(8,128)(2,1)S(1)} %slice.186), channel_id=1, source_target_pairs={{0,32},{32,0},{1,33},{33,1},{2,34},{34,2},{3,35},{35,3},{4,36},{36... | collective-permute-start | bytes 1376264 | tf_op jit(solution)/shard_map/ppermute | solution.py:18
  76.9 3.7 %collective-permute-start.5 = (bf16[64,3584]{1,0:T(8,128)(2,1)S(1)}, bf16[64,3584]{1,0:T(8,128)(2,1)S(1)}, u32[]{:S(2)}, u32[]{:S(2)}) collective-permute-start(bf16[64,3584]{1,0:T(8,128)(2,1)S(1)} %collective-permute-done.4), channel_id=1, source_target_pairs={{0,32},{32,0},{1,33},{33,1},{2,34},{34,2},{3,35},{35,3},{4,36},{36... | collective-permute-start | bytes 1376264 | tf_op jit(solution)/shard_map/ppermute | solution.py:18
  81.9 5.9 %collective-permute-start.10 = (bf16[64,3584]{1,0:T(8,128)(2,1)S(1)}, bf16[64,3584]{1,0:T(8,128)(2,1)S(1)}, u32[]{:S(2)}, u32[]{:S(2)}) collective-permute-start(bf16[64,3584]{1,0:T(8,128)(2,1)S(1)} %slice.185), channel_id=1, source_target_pairs={{0,32},{32,0},{1,33},{33,1},{2,34},{34,2},{3,35},{35,3},{4,36},{36... | collective-permute-start | bytes 1376264 | tf_op jit(solution)/shard_map/ppermute | solution.py:18
  85.5 6.4 %collective-permute-start.7 = (bf16[128,3584]{1,0:T(8,128)(2,1)S(1)}, bf16[128,3584]{1,0:T(8,128)(2,1)S(1)}, u32[]{:S(2)}, u32[]{:S(2)}) collective-permute-start(bf16[128,3584]{1,0:T(8,128)(2,1)S(1)} %slice.184), channel_id=1, source_target_pairs={{0,32},{32,0},{1,33},{33,1},{2,34},{34,2},{3,35},{35,3},{4,36},{36... | collective-permute-start | bytes 2752520 | tf_op jit(solution)/shard_map/ppermute | solution.py:18
  87.9 16.8 %collective-permute-start.11 = (bf16[64,3584]{1,0:T(8,128)(2,1)S(1)}, bf16[64,3584]{1,0:T(8,128)(2,1)S(1)}, u32[]{:S(2)}, u32[]{:S(2)}) collective-permute-start(bf16[64,3584]{1,0:T(8,128)(2,1)S(1)} %fusion.7), channel_id=1, source_target_pairs={{0,256},{128,384},{256,0},{384,128},{1,257},{129,385},{257,1},{385... | collective-permute-start | bytes 1376264 | tf_op jit(solution)/shard_map/ppermute | solution.py:13
  92.2 20.7 %collective-permute-start.8 = (bf16[64,3584]{1,0:T(8,128)(2,1)S(1)}, bf16[64,3584]{1,0:T(8,128)(2,1)S(1)}, u32[]{:S(2)}, u32[]{:S(2)}) collective-permute-start(bf16[64,3584]{1,0:T(8,128)(2,1)S(1)} %get-tuple-element.10), channel_id=1, source_target_pairs={{0,384},{128,0},{256,128},{384,256},{1,385},{129,1},{257,129},{385... | collective-permute-start | bytes 1376264 | tf_op jit(solution)/shard_map/ppermute | solution.py:13
  95.1 18.5 %collective-permute-start.9 = (bf16[64,3584]{1,0:T(8,128)(2,1)S(1)}, bf16[64,3584]{1,0:T(8,128)(2,1)S(1)}, u32[]{:S(2)}, u32[]{:S(2)}) collective-permute-start(bf16[64,3584]{1,0:T(8,128)(2,1)S(1)} %get-tuple-element.11), channel_id=1, source_target_pairs={{0,128},{128,256},{256,384},{384,0},{1,129},{129,257},{257,385},{3... | collective-permute-start | bytes 1376264 | tf_op jit(solution)/shard_map/ppermute | solution.py:13
  101.6 20.4 %collective-permute-start.12 = (f32[1]{0:T(128)}, f32[1]{0:T(128)}, u32[]{:S(2)}, u32[]{:S(2)}) collective-permute-start(f32[1]{0:T(128)} %bitcast.49), channel_id=1, source_target_pairs={{0,32},{32,0},{1,33},{33,1},{2,34},{34,2},{3,35},{35,3},{4,36},{36... | collective-permute-start | bytes 20 | tf_op jit(solution)/shard_map/ppermute | solution.py:18
  114.8 22.4 %all-to-all-start.1 = ((bf16[4,64,896]{2,1,0:T(8,128)(2,1)}), bf16[4,64,896]{2,1,0:T(8,128)(2,1)S(1)}, u32[]{:S(2)}, u32[]{:S(2)}) async-start(bf16[4,64,896]{2,1,0:T(8,128)(2,1)} %pad_maximum_fusion.3), calls=%async_computation.1 | async-start | bytes 917504 | tf_op jit(solution)/shard_map/all_to_all | solution.py:113
  123.3 5.6 %collective-permute-start.13 = (f32[1]{0:T(128)}, f32[1]{0:T(128)}, u32[]{:S(2)}, u32[]{:S(2)}) collective-permute-start(f32[1]{0:T(128)} %add.131), channel_id=1, source_target_pairs={{0,128},{128,0},{256,384},{384,256},{1,129},{129,1},{257,385},{385... | collective-permute-start | bytes 20 | tf_op jit(solution)/shard_map/ppermute | solution.py:18
  129.5 7.1 %collective-permute-start.14 = (f32[1]{0:T(128)}, f32[1]{0:T(128)}, u32[]{:S(2)}, u32[]{:S(2)}) collective-permute-start(f32[1]{0:T(128)} %add.132), channel_id=1, source_target_pairs={{0,256},{128,384},{256,0},{384,128},{1,257},{129,385},{257,1},{385... | collective-permute-start | bytes 20 | tf_op jit(solution)/shard_map/ppermute | solution.py:18
  138.3 18.5 %collective-permute-start.15 = (f32[1]{0:T(128)}, f32[1]{0:T(128)}, u32[]{:S(2)}, u32[]{:S(2)}) collective-permute-start(f32[1]{0:T(128)} %add.133), channel_id=1, source_target_pairs={{0,64},{64,0},{1,65},{65,1},{2,66},{66,2},{3,67},{67,3},{4,68},{68... | collective-permute-start | bytes 20 | tf_op jit(solution)/shard_map/ppermute | solution.py:18
  149.1 27.7 %all-to-all-start.2 = ((bf16[16,112,96]{1,2,0:T(8,128)(2,1)}), bf16[16,112,96]{1,2,0:T(8,128)(2,1)S(1)}, u32[]{:S(2)}, u32[]{:S(2)}) async-start(bf16[16,112,96]{1,2,0:T(8,128)(2,1)} %copy.123), calls=%async_computation.2 | async-start | bytes 786432 | tf_op jit(solution)/shard_map/all_to_all | solution.py:128
where the time goes:
time: 178 us
  starting transfers between devices  73 us (41%)
  waiting for transfers between devices  41.9 us (24%)
  blocking collectives  35.6 us (20%)
  local copies, waits for them, and re-layouts  8.13 us (5%)
  matrix products  7.87 us (4%)
  other arithmetic  5.87 us (3%)
  between operations  5.27 us (3%)
    all_gather x1, blocking collectives, body(): along_z = lax.all_gather(tokens.T, ('zh', 'zl'), axis=0, tiled=True)  35.6 us
    ppermute x10, starting transfers between devices, swap(): return lax.ppermute(value, axis, [(i, i ^ bit) for i in range(size)])  33.4 us
    ppermute x6, starting transfers between devices, shift(): lax.ppermute(value, axis, [(i, (i + step) % size) for i in range(size)])  20.7 us
    ppermute x6, waiting for transfers between devices, shift(): lax.ppermute(value, axis, [(i, (i + step) % size) for i in range(size)])  16.8 us
    all_to_all x1, waiting for transfers between devices, body(): landed = lax.all_to_all(sent, ('zh', 'zl'), 0, 0, tiled=True)  14.9 us
    all_to_all x1, starting transfers between devices, body(): landed = lax.all_to_all(sent, ('zh', 'zl'), 0, 0, tiled=True)  7.67 us
    all_to_all x1, starting transfers between devices, body(): back = lax.all_to_all(back, 'x', 0, 0, tiled=True)  6.4 us
    ppermute x10, waiting for transfers between devices, swap(): return lax.ppermute(value, axis, [(i, i ^ bit) for i in range(size)])  5.49 us
  transfers between devices with their start and end apart: 19, of which 10 were waited for; matrix products, arithmetic and copies ran while one was open for 9% of the time, Pallas kernels for 0%

commit v1 on v0

--- a/solution.py
+++ b/solution.py
@@ -27,14 +27,14 @@
     own = lax.dynamic_index_in_dim(blocks, yi, 0, keepdims=False)
     own = lax.dynamic_index_in_dim(own, ci, 1, keepdims=False)
     experts = zli * n_x + jnp.arange(n_x, dtype=jnp.int32)
-    named = jnp.any(own[:, None, :, :] == experts[None, :, None, None], axis=3)
+    chosen = jnp.any(own[:, None, :, :] == experts[None, :, None, None], axis=3)
     row = lax.broadcasted_iota(jnp.int32, (tok, tok), 0)
     col = lax.broadcasted_iota(jnp.int32, (tok, tok), 1)
     earlier = (row < col).astype(BF)
     rank = lax.dot_general(
-        named.astype(BF), earlier, (((2,), (0,)), ((), ())), preferred_element_type=F32
+        chosen.astype(BF), earlier, (((2,), (0,)), ((), ())), preferred_element_type=F32
     )
-    rank = jnp.where(named, rank, -1.0)
+    rank = jnp.where(chosen, rank, -1.0)
     slots = lax.broadcasted_iota(jnp.int32, (1, 1, cap, 1), 2).astype(F32)
     return (rank[:, :, None, :] == slots).astype(BF)
 
@@ -68,8 +68,10 @@
     arrived = lax.all_to_all(outgoing, "x", 0, 0, tiled=True)
     own = jnp.concatenate([arrived[j] for j in range(n_x)], axis=1)
 
-    a1, a3, a2 = shift(own, "y", 1), shift(own, "y", -1), shift(own, "y", 2)
-    a_of = {(0,): own, (1, 3): jnp.concatenate([a1, a3], axis=0), (2,): a2}
+    a2 = shift(own, "y", 2)
+    a1 = shift(own, "y", 1)
+    a3 = shift(own, "y", -1)
+    a_of = {(0,): own, (1, 3, 2): jnp.concatenate([a1, a3, a2], axis=0)}
 
     grads = hidden_grad[0].reshape(n_y, 2, 2, cap, units).transpose(0, 2, 1, 3, 4)
 
@@ -93,9 +95,10 @@
         return jnp.where(ci == 0, both, both[::-1]).reshape(-1, units)
 
     x_list, act_list, hidden_of, summed = [], [], {}, {}
-    for group in ((0,), (1, 3), (2,)):
+    for group in ((0,), (1, 3, 2)):
         count = len(group) * rows
-        x_rows = jnp.concatenate([a_of[group], swap(a_of[group], "core", 1)], axis=0)
+        twin = swap(a_of[group], "core", 1)
+        x_rows = jnp.concatenate([a_of[group], twin], axis=0)
         hid, act, partial = math(x_rows, grad_rows_of(group))
         x_list.append(x_rows)
         act_list.append(act)
@@ -106,8 +109,20 @@
             hidden_of[r] = hid[:, n]
             summed[r] = both[n * rows : (n + 1) * rows]
 
-    got = [shift(summed[r].astype(BF), "y", -r).astype(F32) for r in (1, 3, 2)]
-    slot_grad = (summed[0] + got[0] + got[1] + got[2]).astype(BF)
+    got = []
+    for r in (1, 3, 2):
+        got.append(shift(summed[r].astype(BF), "y", -r).astype(F32))
+
+    x_all = jnp.concatenate(x_list, axis=0)
+    act_all = jnp.concatenate(act_list, axis=0)
+    raw = lax.dot_general(x_all, act_all, (((0,), (0,)), ((), ())), preferred_element_type=F32)
+    total = jnp.sum(raw * raw).reshape(1)
+    other_half = swap(total, "zh", 1)
+    total = total + other_half
+    total = total + swap(total, "core", 1)
+
+    base, total = lax.optimization_barrier((summed[0], total))
+    slot_grad = (base + got[0] + got[1] + got[2]).astype(BF)
 
     back = jnp.stack([slot_grad[:, j * part : (j + 1) * part] for j in range(n_x)])
     back = lax.all_to_all(back, "x", 0, 0, tiled=True)
@@ -116,19 +131,12 @@
         back, onehot, (((1,), (1,)), ((0,), (0,))), preferred_element_type=F32
     ).reshape(n_z, feat, tok)
 
-    x_all = jnp.concatenate(x_list, axis=0)
-    act_all = jnp.concatenate(act_list, axis=0)
-    raw = lax.dot_general(x_all, act_all, (((0,), (0,)), ((), ())), preferred_element_type=F32)
-    total = jnp.sum(raw * raw).reshape(1)
-    total = total + swap(total, "core", 1)
-    total = total + swap(total, "y", 1)
-    total = total + swap(total, "y", 2)
-
     sent, total = lax.optimization_barrier((token_sum.astype(BF), total))
     landed = lax.all_to_all(sent, ("zh", "zl"), 0, 0, tiled=True)
     token_grad = jnp.sum(landed.astype(F32), axis=0).astype(BF).T
-    other_half = swap(total, "zh", 1)
-    total = total + other_half
+    other = swap(total, "y", 1)
+    total = total + other
+    total = total + swap(total, "y", 2)
     root_mean = jnp.sqrt(total / (2.0 * width * units * n_dp) + 1e-06)
     clip_scale = jnp.minimum(1.0, clip_limit / root_mean)
     scaled = (clip_scale[:, None] * raw).astype(BF)

time: 178 us -> 170 us (0.955)
  the two profiles are of different devices: /device:TPU:36 before, /device:TPU:16 now
where the time goes in v1:
time: 170 us; the launch traced here: 169 us
  starting transfers between devices  60.8 us (36%)
  waiting for transfers between devices  38.6 us (23%)
  blocking collectives  37.9 us (22%)
  local copies, waits for them, and re-layouts  10.8 us (6%)
  other arithmetic  8.38 us (5%)
  matrix products  7.19 us (4%)
  between operations  4.98 us (3%)
    all_gather x1, blocking collectives, body(): along_z = lax.all_gather(tokens.T, ('zh', 'zl'), axis=0, tiled=True)  37.9 us
    ppermute x8, starting transfers between devices, swap(): return lax.ppermute(value, axis, [(i, i ^ bit) for i in range(size)])  25.2 us
    ppermute x6, starting transfers between devices, shift(): lax.ppermute(value, axis, [(i, (i + step) % size) for i in range(size)])  20.7 us
    ppermute x8, waiting for transfers between devices, swap(): return lax.ppermute(value, axis, [(i, i ^ bit) for i in range(size)])  16.2 us
    all_to_all x1, waiting for transfers between devices, body(): back = lax.all_to_all(back, 'x', 0, 0, tiled=True)  8.57 us
    all_to_all x1, starting transfers between devices, body(): landed = lax.all_to_all(sent, ('zh', 'zl'), 0, 0, tiled=True)  7.14 us
    all_to_all x1, waiting for transfers between devices, body(): arrived = lax.all_to_all(outgoing, 'x', 0, 0, tiled=True)  5.88 us
    all_to_all x1, waiting for transfers between devices, body(): landed = lax.all_to_all(sent, ('zh', 'zl'), 0, 0, tiled=True)  4.36 us
  transfers between devices with their start and end apart: 17, of which 9 were waited for; matrix products, arithmetic and copies ran while one was open for 10% of the time, Pallas kernels for 0%

profile of v1, /device:TPU:16, one launch (start us, length us, event | category | flops | bytes accessed | tf_op | source)
XLA Modules:
  0.0 168.6 jit_solution(12063605245866562932)
XLA Ops:
  2.1 37.9 %all-gather = bf16[16,112,96]{1,2,0:T(8,128)(2,1)S(1)} all-gather(bf16[1,112,96]{1,2,0:T(8,128)(2,1)} %bitcast.135), channel_id=1, replica_groups=mesh['y'=4,'zh'=2,'core'=2,'zl'=8,'x'=4] {'zh','zl'}, dimensions={0}, use_global_device_ids=true | all-gather | bytes 365568 | tf_op jit(solution)/shard_map/all_gather | solution.py:53
  42.2 4.3 %all-to-all-start = ((bf16[4,64,896]{2,1,0:T(8,128)(2,1)}), bf16[4,64,896]{2,1,0:T(8,128)(2,1)S(1)}, u32[]{:S(2)}, u32[]{:S(2)}) async-start(bf16[4,64,896]{2,1,0:T(8,128)(2,1)} %bitcast.7), calls=%async_computation | async-start | bytes 917504 | tf_op jit(solution)/shard_map/all_to_all | solution.py:68
  48.3 5.9 %all-to-all-done = bf16[4,64,896]{2,1,0:T(8,128)(2,1)S(1)} async-done(((bf16[4,64,896]{2,1,0:T(8,128)(2,1)}), bf16[4,64,896]{2,1,0:T(8,128)(2,1)S(1)}, u32[]{:S(2)}, u32[]{:S(2)}) %all-to-all-start) | async-done | bytes 458784 | tf_op jit(solution)/shard_map/all_to_all | solution.py:68
  55.3 2.3 %collective-permute-start.2 = (bf16[64,3584]{1,0:T(8,128)(2,1)}, bf16[64,3584]{1,0:T(8,128)(2,1)S(1)}, u32[]{:S(2)}, u32[]{:S(2)}) collective-permute-start(bf16[64,3584]{1,0:T(8,128)(2,1)} %get-tuple-element.24), channel_id=1, source_target_pairs={{0,384},{128,0},{256,128},{384,256},{1,385},{129,1},{257,129},{385... | collective-permute-start | bytes 1376264 | tf_op jit(solution)/shard_map/ppermute | solution.py:13
  57.6 3.5 %collective-permute-start.1 = (bf16[64,3584]{1,0:T(8,128)(2,1)}, bf16[64,3584]{1,0:T(8,128)(2,1)S(1)}, u32[]{:S(2)}, u32[]{:S(2)}) collective-permute-start(bf16[64,3584]{1,0:T(8,128)(2,1)} %get-tuple-element.24), channel_id=1, source_target_pairs={{0,128},{128,256},{256,384},{384,0},{1,129},{129,257},{257,385},{3... | collective-permute-start | bytes 1376264 | tf_op jit(solution)/shard_map/ppermute | solution.py:13
  61.1 3.2 %collective-permute-start.3 = (bf16[64,3584]{1,0:T(8,128)(2,1)}, bf16[64,3584]{1,0:T(8,128)(2,1)S(1)}, u32[]{:S(2)}, u32[]{:S(2)}) collective-permute-start(bf16[64,3584]{1,0:T(8,128)(2,1)} %get-tuple-element.24), channel_id=1, source_target_pairs={{0,256},{128,384},{256,0},{384,128},{1,257},{129,385},{257,1},{385... | collective-permute-start | bytes 1376264 | tf_op jit(solution)/shard_map/ppermute | solution.py:13
  70.4 3.6 %collective-permute-done.3 = bf16[64,3584]{1,0:T(8,128)(2,1)S(1)} collective-permute-done((bf16[64,3584]{1,0:T(8,128)(2,1)}, bf16[64,3584]{1,0:T(8,128)(2,1)S(1)}, u32[]{:S(2)}, u32[]{:S(2)}) %collective-permute-start.3) | collective-permute-done | bytes 458784 | tf_op jit(solution)/shard_map/ppermute | solution.py:13
  77.4 2.5 %collective-permute-start.5 = (bf16[64,3584]{1,0:T(8,128)(2,1)S(1)}, bf16[64,3584]{1,0:T(8,128)(2,1)S(1)}, u32[]{:S(2)}, u32[]{:S(2)}) collective-permute-start(bf16[64,3584]{1,0:T(8,128)(2,1)S(1)} %slice.162), channel_id=1, source_target_pairs={{0,32},{32,0},{1,33},{33,1},{2,34},{34,2},{3,35},{35,3},{4,36},{36... | collective-permute-start | bytes 1376264 | tf_op jit(solution)/shard_map/ppermute | solution.py:18
  84.3 2.9 %collective-permute-done.8 = bf16[192,3584]{1,0:T(8,128)(2,1)S(1)} collective-permute-done((bf16[192,3584]{1,0:T(8,128)(2,1)S(1)}, bf16[192,3584]{1,0:T(8,128)(2,1)S(1)}, u32[]{:S(2)}, u32[]{:S(2)}) %collective-permute-start.8) | collective-permute-done | bytes 1376288 | tf_op jit(solution)/shard_map/ppermute | solution.py:18
  89.5 5.7 %collective-permute-start.11 = (bf16[64,3584]{1,0:T(8,128)(2,1)S(1)}, bf16[64,3584]{1,0:T(8,128)(2,1)S(1)}, u32[]{:S(2)}, u32[]{:S(2)}) collective-permute-start(bf16[64,3584]{1,0:T(8,128)(2,1)S(1)} %get-tuple-element.15), channel_id=1, source_target_pairs={{0,256},{128,384},{256,0},{384,128},{1,257},{129,385},{257,1},{385... | collective-permute-start | bytes 1376264 | tf_op jit(solution)/shard_map/ppermute | solution.py:13
  95.2 3.9 %collective-permute-start.10 = (bf16[64,3584]{1,0:T(8,128)(2,1)S(1)}, bf16[64,3584]{1,0:T(8,128)(2,1)S(1)}, u32[]{:S(2)}, u32[]{:S(2)}) collective-permute-start(bf16[64,3584]{1,0:T(8,128)(2,1)S(1)} %get-tuple-element.16), channel_id=1, source_target_pairs={{0,128},{128,256},{256,384},{384,0},{1,129},{129,257},{257,385},{3... | collective-permute-start | bytes 1376264 | tf_op jit(solution)/shard_map/ppermute | solution.py:13
  99.1 3.5 %multiply_reduce_fusion = (f32[]{:T(128)}, f32[3584,256]{1,0:T(8,128)}) fusion(bf16[512,3584]{1,0:T(8,128)(2,1)S(1)} %constant_dynamic-update-slice_fusion, bf16[384,128]{1,0:T(8,128)(2,1)S(1)} %get-tuple-element.18, bf16[384,128]{1,0:T(8,128)(2,1)S(1)} %get-tuple-element.17, bf16[128,128]{1,0:T(8,128)(2,1)S(1)} %get-tuple-element.31, ...), kind=kOutput, calls=%fused_computation.1 | convolution fusion | flops 942407680 | bytes 7602180 | tf_op jit(solution)/shard_map/dot_general | solution.py:118
  102.7 7.7 %collective-permute-start.6 = (f32[1]{0:T(128)}, f32[1]{0:T(128)}, u32[]{:S(2)}, u32[]{:S(2)}) collective-permute-start(f32[1]{0:T(128)} %bitcast.37), channel_id=1, source_target_pairs={{0,64},{64,0},{1,65},{65,1},{2,66},{66,2},{3,67},{67,3},{4,68},{68... | collective-permute-start | bytes 20 | tf_op jit(solution)/shard_map/ppermute | solution.py:18
  110.4 6.7 %collective-permute-done.6 = f32[1]{0:T(128)} collective-permute-done((f32[1]{0:T(128)}, f32[1]{0:T(128)}, u32[]{:S(2)}, u32[]{:S(2)}) %collective-permute-start.6) | collective-permute-done | bytes 36 | tf_op jit(solution)/shard_map/ppermute | solution.py:18
  118.3 2.9 %collective-permute-start.7 = (f32[1]{0:T(128)}, f32[1]{0:T(128)}, u32[]{:S(2)}, u32[]{:S(2)}) collective-permute-start(f32[1]{0:T(128)} %add.115), channel_id=1, source_target_pairs={{0,32},{32,0},{1,33},{33,1},{2,34},{34,2},{3,35},{35,3},{4,36},{36... | collective-permute-start | bytes 20 | tf_op jit(solution)/shard_map/ppermute | solution.py:18
  123.3 3.5 %all-to-all-start.1 = ((bf16[4,64,896]{2,1,0:T(8,128)(2,1)}), bf16[4,64,896]{2,1,0:T(8,128)(2,1)S(1)}, u32[]{:S(2)}, u32[]{:S(2)}) async-start(bf16[4,64,896]{2,1,0:T(8,128)(2,1)} %pad_maximum_fusion.3), calls=%async_computation.1 | async-start | bytes 917504 | tf_op jit(solution)/shard_map/all_to_all | solution.py:128
  127.6 8.6 %all-to-all-done.1 = bf16[4,64,896]{2,1,0:T(8,128)(2,1)S(1)} async-done(((bf16[4,64,896]{2,1,0:T(8,128)(2,1)}), bf16[4,64,896]{2,1,0:T(8,128)(2,1)S(1)}, u32[]{:S(2)}, u32[]{:S(2)}) %all-to-all-start.1) | async-done | bytes 458784 | tf_op jit(solution)/shard_map/all_to_all | solution.py:128
  138.1 7.1 %all-to-all-start.2 = ((bf16[16,112,96]{1,2,0:T(8,128)(2,1)}), bf16[16,112,96]{1,2,0:T(8,128)(2,1)S(1)}, u32[]{:S(2)}, u32[]{:S(2)}) async-start(bf16[16,112,96]{1,2,0:T(8,128)(2,1)} %copy.123), calls=%async_computation.2 | async-start | bytes 786432 | tf_op jit(solution)/shard_map/all_to_all | solution.py:135
  145.3 3.2 %collective-permute-start.12 = (f32[1]{0:T(128)}, f32[1]{0:T(128)}, u32[]{:S(2)}, u32[]{:S(2)}) collective-permute-start(f32[1]{0:T(128)} %add.116), channel_id=1, source_target_pairs={{0,128},{128,0},{256,384},{384,256},{1,129},{129,1},{257,385},{385... | collective-permute-start | bytes 20 | tf_op jit(solution)/shard_map/ppermute | solution.py:18
  148.5 2.4 %collective-permute-done.12 = f32[1]{0:T(128)} collective-permute-done((f32[1]{0:T(128)}, f32[1]{0:T(128)}, u32[]{:S(2)}, u32[]{:S(2)}) %collective-permute-start.12) | collective-permute-done | bytes 36 | tf_op jit(solution)/shard_map/ppermute | solution.py:18
  151.4 3.2 %collective-permute-start.13 = (f32[1]{0:T(128)}, f32[1]{0:T(128)}, u32[]{:S(2)}, u32[]{:S(2)}) collective-permute-start(f32[1]{0:T(128)} %add.121), channel_id=1, source_target_pairs={{0,256},{128,384},{256,0},{384,128},{1,257},{129,385},{257,1},{385... | collective-permute-start | bytes 20 | tf_op jit(solution)/shard_map/ppermute | solution.py:18
  154.6 3.9 %collective-permute-done.13 = f32[1]{0:T(128)} collective-permute-done((f32[1]{0:T(128)}, f32[1]{0:T(128)}, u32[]{:S(2)}, u32[]{:S(2)}) %collective-permute-start.13) | collective-permute-done | bytes 36 | tf_op jit(solution)/shard_map/ppermute | solution.py:18
  159.1 2.3 %multiply_convert_fusion = bf16[3584,256]{1,0:T(8,128)(2,1)S(1)} fusion(f32[3584,256]{1,0:T(8,128)} %get-tuple-element.42, f32[]{:T(128)} %bitcast.45), kind=kLoop, calls=%fused_computation | loop fusion | flops 1835008 | bytes 5505028 | tf_op jit(solution)/shard_map/convert_element_type | solution.py:142
  163.5 4.4 %all-to-all-done.2 = bf16[16,112,96]{1,2,0:T(8,128)(2,1)S(1)} async-done(((bf16[16,112,96]{1,2,0:T(8,128)(2,1)}), bf16[16,112,96]{1,2,0:T(8,128)(2,1)S(1)}, u32[]{:S(2)}, u32[]{:S(2)}) %all-to-all-start.2) | async-done | bytes 344096 | tf_op jit(solution)/shard_map/all_to_all | solution.py:135
  (92 shorter events, 28.5 us)
Async XLA Ops:
  0.6 45.8 %copy-start.6 = (bf16[1,16,32,128]{3,2,1,0:T(8,128)(2,1)S(1)}, bf16[1,16,32,128]{3,2,1,0:T(8,128)(2,1)}, u32[]{:S(2)}) copy-start(bf16[1,16,32,128]{3,2,1,0:T(8,128)(2,1)} %param.10) | copy-start | bytes 393220
  41.0 1.2 copy-start.4
  41.4 26.9 %copy-start = (bf16[1,3584,128]{2,1,0:T(8,128)(2,1)S(1)}, bf16[1,3584,128]{2,1,0:T(8,128)(2,1)}, u32[]{:S(2)}) copy-start(bf16[1,3584,128]{2,1,0:T(8,128)(2,1)} %param.8) | copy-start | bytes 2752516
  42.2 12.0 %all-to-all-start = ((bf16[4,64,896]{2,1,0:T(8,128)(2,1)}), bf16[4,64,896]{2,1,0:T(8,128)(2,1)S(1)}, u32[]{:S(2)}, u32[]{:S(2)}) async-start(bf16[4,64,896]{2,1,0:T(8,128)(2,1)} %bitcast.7), calls=%async_computation | async-start | bytes 917504 | tf_op jit(solution)/shard_map/all_to_all | solution.py:68
  46.5 21.9 %copy-start.1 = (bf16[1,3584,128]{2,1,0:T(8,128)(2,1)S(1)}, bf16[1,3584,128]{2,1,0:T(8,128)(2,1)}, u32[]{:S(2)}) copy-start(bf16[1,3584,128]{2,1,0:T(8,128)(2,1)} %param.9) | copy-start | bytes 2752516
  55.3 15.1 %collective-permute-start.2 = (bf16[64,3584]{1,0:T(8,128)(2,1)}, bf16[64,3584]{1,0:T(8,128)(2,1)S(1)}, u32[]{:S(2)}, u32[]{:S(2)}) collective-permute-start(bf16[64,3584]{1,0:T(8,128)(2,1)} %get-tuple-element.24), channel_id=1, source_target_pairs={{0,384},{128,0},{256,128},{384,256},{1,385},{129,1},{257,129},{385... | collective-permute-start | bytes 1376264 | tf_op jit(solution)/shard_map/ppermute | solution.py:13
  57.6 12.8 %collective-permute-start.1 = (bf16[64,3584]{1,0:T(8,128)(2,1)}, bf16[64,3584]{1,0:T(8,128)(2,1)S(1)}, u32[]{:S(2)}, u32[]{:S(2)}) collective-permute-start(bf16[64,3584]{1,0:T(8,128)(2,1)} %get-tuple-element.24), channel_id=1, source_target_pairs={{0,128},{128,256},{256,384},{384,0},{1,129},{129,257},{257,385},{3... | collective-permute-start | bytes 1376264 | tf_op jit(solution)/shard_map/ppermute | solution.py:13
  61.1 12.9 %collective-permute-start.3 = (bf16[64,3584]{1,0:T(8,128)(2,1)}, bf16[64,3584]{1,0:T(8,128)(2,1)S(1)}, u32[]{:S(2)}, u32[]{:S(2)}) collective-permute-start(bf16[64,3584]{1,0:T(8,128)(2,1)} %get-tuple-element.24), channel_id=1, source_target_pairs={{0,256},{128,384},{256,0},{384,128},{1,257},{129,385},{257,1},{385... | collective-permute-start | bytes 1376264 | tf_op jit(solution)/shard_map/ppermute | solution.py:13
  68.3 7.7 %copy-start.3 = (bf16[64,896]{1,0:T(8,128)(2,1)S(1)}, bf16[64,896]{1,0:T(8,128)(2,1)}, u32[]{:S(2)}) copy-start(bf16[64,896]{1,0:T(8,128)(2,1)} %copy-done.2) | copy-start | bytes 344068
  68.4 7.6 %collective-permute-start = (bf16[64,3584]{1,0:T(8,128)(2,1)}, bf16[64,3584]{1,0:T(8,128)(2,1)S(1)}, u32[]{:S(2)}, u32[]{:S(2)}) collective-permute-start(bf16[64,3584]{1,0:T(8,128)(2,1)} %get-tuple-element.24), channel_id=1, source_target_pairs={{0,32},{32,0},{1,33},{33,1},{2,34},{34,2},{3,35},{35,3},{4,36},{36... | collective-permute-start | bytes 1376264 | tf_op jit(solution)/shard_map/ppermute | solution.py:18
  74.1 6.0 %collective-permute-start.4 = (bf16[192,3584]{1,0:T(8,128)(2,1)S(1)}, bf16[192,3584]{1,0:T(8,128)(2,1)S(1)}, u32[]{:S(2)}, u32[]{:S(2)}) collective-permute-start(bf16[192,3584]{1,0:T(8,128)(2,1)S(1)} %pad_maximum_fusion.1), channel_id=1, source_target_pairs={{0,32},{32,0},{1,33},{33,1},{2,34},{34,2},{3,35},{35,3},{4,36},{36... | collective-permute-start | bytes 4128776 | tf_op jit(solution)/shard_map/ppermute | solution.py:18
  76.5 3.4 %copy-start.7 = (bf16[512,3584]{1,0:T(8,128)(2,1)S(1)}, bf16[512,3584]{1,0:T(8,128)(2,1)}, u32[]{:S(2)}) copy-start(bf16[512,3584]{1,0:T(8,128)(2,1)} %get-tuple-element.23) | copy-start | bytes 11010052
  77.4 6.7 %collective-permute-start.5 = (bf16[64,3584]{1,0:T(8,128)(2,1)S(1)}, bf16[64,3584]{1,0:T(8,128)(2,1)S(1)}, u32[]{:S(2)}, u32[]{:S(2)}) collective-permute-start(bf16[64,3584]{1,0:T(8,128)(2,1)S(1)} %slice.162), channel_id=1, source_target_pairs={{0,32},{32,0},{1,33},{33,1},{2,34},{34,2},{3,35},{35,3},{4,36},{36... | collective-permute-start | bytes 1376264 | tf_op jit(solution)/shard_map/ppermute | solution.py:18
  82.2 5.0 %collective-permute-start.8 = (bf16[192,3584]{1,0:T(8,128)(2,1)S(1)}, bf16[192,3584]{1,0:T(8,128)(2,1)S(1)}, u32[]{:S(2)}, u32[]{:S(2)}) collective-permute-start(bf16[192,3584]{1,0:T(8,128)(2,1)S(1)} %slice.161), channel_id=1, source_target_pairs={{0,32},{32,0},{1,33},{33,1},{2,34},{34,2},{3,35},{35,3},{4,36},{36... | collective-permute-start | bytes 4128776 | tf_op jit(solution)/shard_map/ppermute | solution.py:18
  87.5 34.6 %collective-permute-start.9 = (bf16[64,3584]{1,0:T(8,128)(2,1)S(1)}, bf16[64,3584]{1,0:T(8,128)(2,1)S(1)}, u32[]{:S(2)}, u32[]{:S(2)}) collective-permute-start(bf16[64,3584]{1,0:T(8,128)(2,1)S(1)} %get-tuple-element.14), channel_id=1, source_target_pairs={{0,384},{128,0},{256,128},{384,256},{1,385},{129,1},{257,129},{385... | collective-permute-start | bytes 1376264 | tf_op jit(solution)/shard_map/ppermute | solution.py:13
  89.5 32.7 %collective-permute-start.11 = (bf16[64,3584]{1,0:T(8,128)(2,1)S(1)}, bf16[64,3584]{1,0:T(8,128)(2,1)S(1)}, u32[]{:S(2)}, u32[]{:S(2)}) collective-permute-start(bf16[64,3584]{1,0:T(8,128)(2,1)S(1)} %get-tuple-element.15), channel_id=1, source_target_pairs={{0,256},{128,384},{256,0},{384,128},{1,257},{129,385},{257,1},{385... | collective-permute-start | bytes 1376264 | tf_op jit(solution)/shard_map/ppermute | solution.py:13
  95.2 27.0 %collective-permute-start.10 = (bf16[64,3584]{1,0:T(8,128)(2,1)S(1)}, bf16[64,3584]{1,0:T(8,128)(2,1)S(1)}, u32[]{:S(2)}, u32[]{:S(2)}) collective-permute-start(bf16[64,3584]{1,0:T(8,128)(2,1)S(1)} %get-tuple-element.16), channel_id=1, source_target_pairs={{0,128},{128,256},{256,384},{384,0},{1,129},{129,257},{257,385},{3... | collective-permute-start | bytes 1376264 | tf_op jit(solution)/shard_map/ppermute | solution.py:13
  102.7 14.4 %collective-permute-start.6 = (f32[1]{0:T(128)}, f32[1]{0:T(128)}, u32[]{:S(2)}, u32[]{:S(2)}) collective-permute-start(f32[1]{0:T(128)} %bitcast.37), channel_id=1, source_target_pairs={{0,64},{64,0},{1,65},{65,1},{2,66},{66,2},{3,67},{67,3},{4,68},{68... | collective-permute-start | bytes 20 | tf_op jit(solution)/shard_map/ppermute | solution.py:18
  118.3 3.2 %collective-permute-start.7 = (f32[1]{0:T(128)}, f32[1]{0:T(128)}, u32[]{:S(2)}, u32[]{:S(2)}) collective-permute-start(f32[1]{0:T(128)} %add.115), channel_id=1, source_target_pairs={{0,32},{32,0},{1,33},{33,1},{2,34},{34,2},{3,35},{35,3},{4,36},{36... | collective-permute-start | bytes 20 | tf_op jit(solution)/shard_map/ppermute | solution.py:18
  122.4 13.8 %copy-start.5 = (pred[2,128,96]{1,2,0:T(32,128)(4,1)S(1)}, pred[2,128,96]{1,2,0:T(32,128)(4,1)}, u32[]{:S(2)}) copy-start(pred[2,128,96]{1,2,0:T(32,128)(4,1)} %copy-done.4) | copy-start | bytes 73732
  123.3 12.8 %all-to-all-start.1 = ((bf16[4,64,896]{2,1,0:T(8,128)(2,1)}), bf16[4,64,896]{2,1,0:T(8,128)(2,1)S(1)}, u32[]{:S(2)}, u32[]{:S(2)}) async-start(bf16[4,64,896]{2,1,0:T(8,128)(2,1)} %pad_maximum_fusion.3), calls=%async_computation.1 | async-start | bytes 917504 | tf_op jit(solution)/shard_map/all_to_all | solution.py:128
  138.1 29.8 %all-to-all-start.2 = ((bf16[16,112,96]{1,2,0:T(8,128)(2,1)}), bf16[16,112,96]{1,2,0:T(8,128)(2,1)S(1)}, u32[]{:S(2)}, u32[]{:S(2)}) async-start(bf16[16,112,96]{1,2,0:T(8,128)(2,1)} %copy.123), calls=%async_computation.2 | async-start | bytes 786432 | tf_op jit(solution)/shard_map/all_to_all | solution.py:135
  145.3 5.6 %collective-permute-start.12 = (f32[1]{0:T(128)}, f32[1]{0:T(128)}, u32[]{:S(2)}, u32[]{:S(2)}) collective-permute-start(f32[1]{0:T(128)} %add.116), channel_id=1, source_target_pairs={{0,128},{128,0},{256,384},{384,256},{1,129},{129,1},{257,385},{385... | collective-permute-start | bytes 20 | tf_op jit(solution)/shard_map/ppermute | solution.py:18
  151.4 7.1 %collective-permute-start.13 = (f32[1]{0:T(128)}, f32[1]{0:T(128)}, u32[]{:S(2)}, u32[]{:S(2)}) collective-permute-start(f32[1]{0:T(128)} %add.121), channel_id=1, source_target_pairs={{0,256},{128,384},{256,0},{384,128},{1,257},{129,385},{257,1},{385... | collective-permute-start | bytes 20 | tf_op jit(solution)/shard_map/ppermute | solution.py:18
  (1 other events, 1.0 us)

commit v2 on v1

--- a/solution.py
+++ b/solution.py
@@ -68,12 +68,22 @@
     arrived = lax.all_to_all(outgoing, "x", 0, 0, tiled=True)
     own = jnp.concatenate([arrived[j] for j in range(n_x)], axis=1)
 
+    grads = hidden_grad[0].reshape(n_y, 2, 2, cap, units).transpose(0, 2, 1, 3, 4)
+
+    def grad_rows_of(group):
+        picked = [lax.dynamic_index_in_dim(grads, (yi - r) % n_y, 0) for r in group]
+        both = jnp.concatenate(picked, axis=0).transpose(1, 0, 2, 3, 4)
+        return jnp.where(ci == 0, both, both[::-1]).reshape(-1, units)
+
+    groups = ((0,), (1, 3, 2))
+    own, weights, *grad_rows = lax.optimization_barrier(
+        (own, weights, *[grad_rows_of(group) for group in groups])
+    )
+
     a2 = shift(own, "y", 2)
     a1 = shift(own, "y", 1)
     a3 = shift(own, "y", -1)
     a_of = {(0,): own, (1, 3, 2): jnp.concatenate([a1, a3, a2], axis=0)}
-
-    grads = hidden_grad[0].reshape(n_y, 2, 2, cap, units).transpose(0, 2, 1, 3, 4)
 
     def math(x_rows, grad_rows):
         pre = jnp.dot(x_rows, weights, preferred_element_type=F32)
@@ -89,20 +99,16 @@
         )
         return hidden, act, partial
 
-    def grad_rows_of(group):
-        picked = [lax.dynamic_index_in_dim(grads, (yi - r) % n_y, 0) for r in group]
-        both = jnp.concatenate(picked, axis=0).transpose(1, 0, 2, 3, 4)
-        return jnp.where(ci == 0, both, both[::-1]).reshape(-1, units)
-
     x_list, act_list, hidden_of, summed = [], [], {}, {}
-    for group in ((0,), (1, 3, 2)):
+    for number, group in enumerate(groups):
         count = len(group) * rows
         twin = swap(a_of[group], "core", 1)
         x_rows = jnp.concatenate([a_of[group], twin], axis=0)
-        hid, act, partial = math(x_rows, grad_rows_of(group))
+        hid, act, partial = math(x_rows, grad_rows[number])
         x_list.append(x_rows)
         act_list.append(act)
-        both = partial[:count] + swap(partial[count:].astype(BF), "core", 1).astype(F32)
+        other = swap(partial[count:].astype(BF), "core", 1)
+        both = partial[:count] + other.astype(F32)
         hid = hid.reshape(2, len(group), 2, cap, units)
         hid = jnp.where(ci == 0, hid, hid[::-1])
         for n, r in enumerate(group):
@@ -117,11 +123,8 @@
     act_all = jnp.concatenate(act_list, axis=0)
     raw = lax.dot_general(x_all, act_all, (((0,), (0,)), ((), ())), preferred_element_type=F32)
     total = jnp.sum(raw * raw).reshape(1)
+    base, total = lax.optimization_barrier((summed[0], total))
     other_half = swap(total, "zh", 1)
-    total = total + other_half
-    total = total + swap(total, "core", 1)
-
-    base, total = lax.optimization_barrier((summed[0], total))
     slot_grad = (base + got[0] + got[1] + got[2]).astype(BF)
 
     back = jnp.stack([slot_grad[:, j * part : (j + 1) * part] for j in range(n_x)])
@@ -131,11 +134,12 @@
         back, onehot, (((1,), (1,)), ((0,), (0,))), preferred_element_type=F32
     ).reshape(n_z, feat, tok)
 
-    sent, total = lax.optimization_barrier((token_sum.astype(BF), total))
+    sent, total = lax.optimization_barrier((token_sum.astype(BF), total + other_half))
     landed = lax.all_to_all(sent, ("zh", "zl"), 0, 0, tiled=True)
     token_grad = jnp.sum(landed.astype(F32), axis=0).astype(BF).T
-    other = swap(total, "y", 1)
+    other = swap(total, "core", 1)
     total = total + other
+    total = total + swap(total, "y", 1)
     total = total + swap(total, "y", 2)
     root_mean = jnp.sqrt(total / (2.0 * width * units * n_dp) + 1e-06)
     clip_scale = jnp.minimum(1.0, clip_limit / root_mean)

time: 170 us -> 177 us (1.041)
  the two profiles are of different devices: /device:TPU:16 before, /device:TPU:2 now
where the time goes in v2:
time: 177 us; the launch traced here: 176 us
  starting transfers between devices  63.4 us (36%)
  waiting for transfers between devices  45.9 us (26%)
  blocking collectives  37.9 us (21%)
  local copies, waits for them, and re-layouts  10.3 us (6%)
  matrix products  7.21 us (4%)
  other arithmetic  6.4 us (4%)
  between operations  4.97 us (3%)
    all_gather x1, blocking collectives, body(): along_z = lax.all_gather(tokens.T, ('zh', 'zl'), axis=0, tiled=True)  37.9 us
    ppermute x8, starting transfers between devices, swap(): return lax.ppermute(value, axis, [(i, i ^ bit) for i in range(size)])  25.1 us
    ppermute x6, waiting for transfers between devices, shift(): lax.ppermute(value, axis, [(i, (i + step) % size) for i in range(size)])  22 us
    ppermute x6, starting transfers between devices, shift(): lax.ppermute(value, axis, [(i, (i + step) % size) for i in range(size)])  21.8 us
    ppermute x8, waiting for transfers between devices, swap(): return lax.ppermute(value, axis, [(i, i ^ bit) for i in range(size)])  10.7 us
    all_to_all x1, starting transfers between devices, body(): landed = lax.all_to_all(sent, ('zh', 'zl'), 0, 0, tiled=True)  6.71 us
    all_to_all x1, waiting for transfers between devices, body(): landed = lax.all_to_all(sent, ('zh', 'zl'), 0, 0, tiled=True)  6.62 us
    all_to_all x1, starting transfers between devices, body(): back = lax.all_to_all(back, 'x', 0, 0, tiled=True)  4.89 us
  transfers between devices with their start and end apart: 17, of which 12 were waited for; matrix products, arithmetic and copies ran while one was open for 10% of the time, Pallas kernels for 0%

profile of v2, /device:TPU:2, one launch (start us, length us, event | category | flops | bytes accessed | tf_op | source)
XLA Modules:
  0.0 176.1 jit_solution(12856436950825484636)
XLA Ops:
  2.2 37.9 %all-gather = bf16[16,112,96]{1,2,0:T(8,128)(2,1)S(1)} all-gather(bf16[1,112,96]{1,2,0:T(8,128)(2,1)} %bitcast.116), channel_id=1, replica_groups=mesh['y'=4,'zh'=2,'core'=2,'zl'=8,'x'=4] {'zh','zl'}, dimensions={0}, use_global_device_ids=true | all-gather | bytes 365568 | tf_op jit(solution)/shard_map/all_gather | solution.py:53
  42.2 4.8 %all-to-all-start = ((bf16[4,64,896]{2,1,0:T(8,128)(2,1)}), bf16[4,64,896]{2,1,0:T(8,128)(2,1)S(1)}, u32[]{:S(2)}, u32[]{:S(2)}) async-start(bf16[4,64,896]{2,1,0:T(8,128)(2,1)} %bitcast.7), calls=%async_computation | async-start | bytes 917504 | tf_op jit(solution)/shard_map/all_to_all | solution.py:68
  55.3 3.5 %collective-permute-start.1 = (bf16[64,3584]{1,0:T(8,128)(2,1)S(1)}, bf16[64,3584]{1,0:T(8,128)(2,1)S(1)}, u32[]{:S(2)}, u32[]{:S(2)}) collective-permute-start(bf16[64,3584]{1,0:T(8,128)(2,1)S(1)} %pad_maximum_fusion.2), channel_id=1, source_target_pairs={{0,128},{128,256},{256,384},{384,0},{1,129},{129,257},{257,385},{3... | collective-permute-start | bytes 1376264 | tf_op jit(solution)/shard_map/ppermute | solution.py:13
  58.8 3.6 %collective-permute-start.2 = (bf16[64,3584]{1,0:T(8,128)(2,1)S(1)}, bf16[64,3584]{1,0:T(8,128)(2,1)S(1)}, u32[]{:S(2)}, u32[]{:S(2)}) collective-permute-start(bf16[64,3584]{1,0:T(8,128)(2,1)S(1)} %pad_maximum_fusion.2), channel_id=1, source_target_pairs={{0,384},{128,0},{256,128},{384,256},{1,385},{129,1},{257,129},{385... | collective-permute-start | bytes 1376264 | tf_op jit(solution)/shard_map/ppermute | solution.py:13
  62.4 3.9 %collective-permute-start.3 = (bf16[64,3584]{1,0:T(8,128)(2,1)S(1)}, bf16[64,3584]{1,0:T(8,128)(2,1)S(1)}, u32[]{:S(2)}, u32[]{:S(2)}) collective-permute-start(bf16[64,3584]{1,0:T(8,128)(2,1)S(1)} %pad_maximum_fusion.2), channel_id=1, source_target_pairs={{0,256},{128,384},{256,0},{384,128},{1,257},{129,385},{257,1},{385... | collective-permute-start | bytes 1376264 | tf_op jit(solution)/shard_map/ppermute | solution.py:13
  71.4 2.7 %collective-permute-done.2 = bf16[64,3584]{1,0:T(8,128)(2,1)S(1)} collective-permute-done((bf16[64,3584]{1,0:T(8,128)(2,1)S(1)}, bf16[64,3584]{1,0:T(8,128)(2,1)S(1)}, u32[]{:S(2)}, u32[]{:S(2)}) %collective-permute-start.2) | collective-permute-done | bytes 458784 | tf_op jit(solution)/shard_map/ppermute | solution.py:13
  74.1 8.3 %collective-permute-done.3 = bf16[64,3584]{1,0:T(8,128)(2,1)S(1)} collective-permute-done((bf16[64,3584]{1,0:T(8,128)(2,1)S(1)}, bf16[64,3584]{1,0:T(8,128)(2,1)S(1)}, u32[]{:S(2)}, u32[]{:S(2)}) %collective-permute-start.3) | collective-permute-done | bytes 458784 | tf_op jit(solution)/shard_map/ppermute | solution.py:13
  84.6 2.9 %collective-permute-done.4 = bf16[192,3584]{1,0:T(8,128)(2,1)S(1)} collective-permute-done((bf16[192,3584]{1,0:T(8,128)(2,1)S(1)}, bf16[192,3584]{1,0:T(8,128)(2,1)S(1)}, u32[]{:S(2)}, u32[]{:S(2)}) %collective-permute-start.4) | collective-permute-done | bytes 1376288 | tf_op jit(solution)/shard_map/ppermute | solution.py:18
  91.9 2.8 %collective-permute-done.6 = bf16[192,3584]{1,0:T(8,128)(2,1)S(1)} collective-permute-done((bf16[192,3584]{1,0:T(8,128)(2,1)S(1)}, bf16[192,3584]{1,0:T(8,128)(2,1)S(1)}, u32[]{:S(2)}, u32[]{:S(2)}) %collective-permute-start.6) | collective-permute-done | bytes 1376288 | tf_op jit(solution)/shard_map/ppermute | solution.py:18
  95.1 5.6 %collective-permute-start.7 = (bf16[64,3584]{1,0:T(8,128)(2,1)S(1)}, bf16[64,3584]{1,0:T(8,128)(2,1)S(1)}, u32[]{:S(2)}, u32[]{:S(2)}) collective-permute-start(bf16[64,3584]{1,0:T(8,128)(2,1)S(1)} %get-tuple-element.22), channel_id=1, source_target_pairs={{0,384},{128,0},{256,128},{384,256},{1,385},{129,1},{257,129},{385... | collective-permute-start | bytes 1376264 | tf_op jit(solution)/shard_map/ppermute | solution.py:13
  102.6 3.4 %collective-permute-start.9 = (bf16[64,3584]{1,0:T(8,128)(2,1)S(1)}, bf16[64,3584]{1,0:T(8,128)(2,1)S(1)}, u32[]{:S(2)}, u32[]{:S(2)}) collective-permute-start(bf16[64,3584]{1,0:T(8,128)(2,1)S(1)} %get-tuple-element.23), channel_id=1, source_target_pairs={{0,256},{128,384},{256,0},{384,128},{1,257},{129,385},{257,1},{385... | collective-permute-start | bytes 1376264 | tf_op jit(solution)/shard_map/ppermute | solution.py:13
  106.0 3.5 %multiply_reduce_fusion = (f32[]{:T(128)}, f32[3584,256]{1,0:T(8,128)}) fusion(bf16[512,3584]{1,0:T(8,128)(2,1)S(1)} %constant_dynamic-update-slice_fusion, bf16[384,128]{1,0:T(8,128)(2,1)S(1)} %get-tuple-element.26, bf16[384,128]{1,0:T(8,128)(2,1)S(1)} %get-tuple-element.25, bf16[128,128]{1,0:T(8,128)(2,1)S(1)} %get-tuple-element.37, ...), kind=kOutput, calls=%fused_computation.1 | convolution fusion | flops 942407680 | bytes 7602180 | tf_op jit(solution)/shard_map/dot_general | solution.py:124
  109.5 7.2 %collective-permute-start.10 = (f32[1]{0:T(128)}, f32[1]{0:T(128)}, u32[]{:S(2)}, u32[]{:S(2)}) collective-permute-start(f32[1]{0:T(128)} %bitcast.36), channel_id=1, source_target_pairs={{0,64},{64,0},{1,65},{65,1},{2,66},{66,2},{3,67},{67,3},{4,68},{68... | collective-permute-start | bytes 20 | tf_op jit(solution)/shard_map/ppermute | solution.py:18
  116.8 3.8 %collective-permute-done.7 = bf16[64,3584]{1,0:T(8,128)(2,1)S(1)} collective-permute-done((bf16[64,3584]{1,0:T(8,128)(2,1)S(1)}, bf16[64,3584]{1,0:T(8,128)(2,1)S(1)}, u32[]{:S(2)}, u32[]{:S(2)}) %collective-permute-start.7) | collective-permute-done | bytes 458784 | tf_op jit(solution)/shard_map/ppermute | solution.py:13
  120.6 5.3 %collective-permute-done.8 = bf16[64,3584]{1,0:T(8,128)(2,1)S(1)} collective-permute-done((bf16[64,3584]{1,0:T(8,128)(2,1)S(1)}, bf16[64,3584]{1,0:T(8,128)(2,1)S(1)}, u32[]{:S(2)}, u32[]{:S(2)}) %collective-permute-start.8) | collective-permute-done | bytes 458784 | tf_op jit(solution)/shard_map/ppermute | solution.py:13
  127.0 4.9 %all-to-all-start.1 = ((bf16[4,64,896]{2,1,0:T(8,128)(2,1)}), bf16[4,64,896]{2,1,0:T(8,128)(2,1)S(1)}, u32[]{:S(2)}, u32[]{:S(2)}) async-start(bf16[4,64,896]{2,1,0:T(8,128)(2,1)} %pad_maximum_fusion.3), calls=%async_computation.1 | async-start | bytes 917504 | tf_op jit(solution)/shard_map/all_to_all | solution.py:131
  133.9 4.8 %all-to-all-done.1 = bf16[4,64,896]{2,1,0:T(8,128)(2,1)S(1)} async-done(((bf16[4,64,896]{2,1,0:T(8,128)(2,1)}), bf16[4,64,896]{2,1,0:T(8,128)(2,1)S(1)}, u32[]{:S(2)}, u32[]{:S(2)}) %all-to-all-start.1) | async-done | bytes 458784 | tf_op jit(solution)/shard_map/all_to_all | solution.py:131
  139.8 2.7 %collective-permute-start.11 = (f32[1]{0:T(128)}, f32[1]{0:T(128)}, u32[]{:S(2)}, u32[]{:S(2)}) collective-permute-start(f32[1]{0:T(128)} %add.119), channel_id=1, source_target_pairs={{0,32},{32,0},{1,33},{33,1},{2,34},{34,2},{3,35},{35,3},{4,36},{36... | collective-permute-start | bytes 20 | tf_op jit(solution)/shard_map/ppermute | solution.py:18
  143.4 6.7 %all-to-all-start.2 = ((bf16[16,112,96]{1,2,0:T(8,128)(2,1)}), bf16[16,112,96]{1,2,0:T(8,128)(2,1)S(1)}, u32[]{:S(2)}, u32[]{:S(2)}) async-start(bf16[16,112,96]{1,2,0:T(8,128)(2,1)} %copy.123), calls=%async_computation.2 | async-start | bytes 786432 | tf_op jit(solution)/shard_map/all_to_all | solution.py:138
  150.7 3.2 %collective-permute-start.12 = (f32[1]{0:T(128)}, f32[1]{0:T(128)}, u32[]{:S(2)}, u32[]{:S(2)}) collective-permute-start(f32[1]{0:T(128)} %add.120), channel_id=1, source_target_pairs={{0,128},{128,0},{256,384},{384,256},{1,129},{129,1},{257,385},{385... | collective-permute-start | bytes 20 | tf_op jit(solution)/shard_map/ppermute | solution.py:18
  156.8 4.2 %collective-permute-start.13 = (f32[1]{0:T(128)}, f32[1]{0:T(128)}, u32[]{:S(2)}, u32[]{:S(2)}) collective-permute-start(f32[1]{0:T(128)} %add.121), channel_id=1, source_target_pairs={{0,256},{128,384},{256,0},{384,128},{1,257},{129,385},{257,1},{385... | collective-permute-start | bytes 20 | tf_op jit(solution)/shard_map/ppermute | solution.py:18
  160.9 2.8 %collective-permute-done.13 = f32[1]{0:T(128)} collective-permute-done((f32[1]{0:T(128)}, f32[1]{0:T(128)}, u32[]{:S(2)}, u32[]{:S(2)}) %collective-permute-start.13) | collective-permute-done | bytes 36 | tf_op jit(solution)/shard_map/ppermute | solution.py:18
  164.4 2.3 %multiply_convert_fusion = bf16[3584,256]{1,0:T(8,128)(2,1)S(1)} fusion(f32[3584,256]{1,0:T(8,128)} %get-tuple-element.48, f32[]{:T(128)} %bitcast.44), kind=kLoop, calls=%fused_computation | loop fusion | flops 1835008 | bytes 5505028 | tf_op jit(solution)/shard_map/convert_element_type | solution.py:146
  168.8 6.6 %all-to-all-done.2 = bf16[16,112,96]{1,2,0:T(8,128)(2,1)S(1)} async-done(((bf16[16,112,96]{1,2,0:T(8,128)(2,1)}), bf16[16,112,96]{1,2,0:T(8,128)(2,1)S(1)}, u32[]{:S(2)}, u32[]{:S(2)}) %all-to-all-start.2) | async-done | bytes 344096 | tf_op jit(solution)/shard_map/all_to_all | solution.py:138
  (81 shorter events, 33.8 us)
Async XLA Ops:
  0.6 46.4 %copy-start = (bf16[1,3584,128]{2,1,0:T(8,128)(2,1)S(1)}, bf16[1,3584,128]{2,1,0:T(8,128)(2,1)}, u32[]{:S(2)}) copy-start(bf16[1,3584,128]{2,1,0:T(8,128)(2,1)} %param.8) | copy-start | bytes 2752516
  41.4 7.9 %copy-start.1 = (bf16[1,16,32,128]{3,2,1,0:T(8,128)(2,1)S(1)}, bf16[1,16,32,128]{3,2,1,0:T(8,128)(2,1)}, u32[]{:S(2)}) copy-start(bf16[1,16,32,128]{3,2,1,0:T(8,128)(2,1)} %param.10) | copy-start | bytes 393220
  42.2 11.1 %all-to-all-start = ((bf16[4,64,896]{2,1,0:T(8,128)(2,1)}), bf16[4,64,896]{2,1,0:T(8,128)(2,1)S(1)}, u32[]{:S(2)}, u32[]{:S(2)}) async-start(bf16[4,64,896]{2,1,0:T(8,128)(2,1)} %bitcast.7), calls=%async_computation | async-start | bytes 917504 | tf_op jit(solution)/shard_map/all_to_all | solution.py:68
  53.4 12.9 %collective-permute-start = (bf16[64,3584]{1,0:T(8,128)(2,1)S(1)}, bf16[64,3584]{1,0:T(8,128)(2,1)S(1)}, u32[]{:S(2)}, u32[]{:S(2)}) collective-permute-start(bf16[64,3584]{1,0:T(8,128)(2,1)S(1)} %pad_maximum_fusion.2), channel_id=1, source_target_pairs={{0,32},{32,0},{1,33},{33,1},{2,34},{34,2},{3,35},{35,3},{4,36},{36... | collective-permute-start | bytes 1376264 | tf_op jit(solution)/shard_map/ppermute | solution.py:18
  55.3 16.1 %collective-permute-start.1 = (bf16[64,3584]{1,0:T(8,128)(2,1)S(1)}, bf16[64,3584]{1,0:T(8,128)(2,1)S(1)}, u32[]{:S(2)}, u32[]{:S(2)}) collective-permute-start(bf16[64,3584]{1,0:T(8,128)(2,1)S(1)} %pad_maximum_fusion.2), channel_id=1, source_target_pairs={{0,128},{128,256},{256,384},{384,0},{1,129},{129,257},{257,385},{3... | collective-permute-start | bytes 1376264 | tf_op jit(solution)/shard_map/ppermute | solution.py:13
  58.8 15.3 %collective-permute-start.2 = (bf16[64,3584]{1,0:T(8,128)(2,1)S(1)}, bf16[64,3584]{1,0:T(8,128)(2,1)S(1)}, u32[]{:S(2)}, u32[]{:S(2)}) collective-permute-start(bf16[64,3584]{1,0:T(8,128)(2,1)S(1)} %pad_maximum_fusion.2), channel_id=1, source_target_pairs={{0,384},{128,0},{256,128},{384,256},{1,385},{129,1},{257,129},{385... | collective-permute-start | bytes 1376264 | tf_op jit(solution)/shard_map/ppermute | solution.py:13
  62.4 20.0 %collective-permute-start.3 = (bf16[64,3584]{1,0:T(8,128)(2,1)S(1)}, bf16[64,3584]{1,0:T(8,128)(2,1)S(1)}, u32[]{:S(2)}, u32[]{:S(2)}) collective-permute-start(bf16[64,3584]{1,0:T(8,128)(2,1)S(1)} %pad_maximum_fusion.2), channel_id=1, source_target_pairs={{0,256},{128,384},{256,0},{384,128},{1,257},{129,385},{257,1},{385... | collective-permute-start | bytes 1376264 | tf_op jit(solution)/shard_map/ppermute | solution.py:13
  67.6 24.1 %collective-permute-start.5 = (bf16[64,3584]{1,0:T(8,128)(2,1)S(1)}, bf16[64,3584]{1,0:T(8,128)(2,1)S(1)}, u32[]{:S(2)}, u32[]{:S(2)}) collective-permute-start(bf16[64,3584]{1,0:T(8,128)(2,1)S(1)} %slice.162), channel_id=1, source_target_pairs={{0,32},{32,0},{1,33},{33,1},{2,34},{34,2},{3,35},{35,3},{4,36},{36... | collective-permute-start | bytes 1376264 | tf_op jit(solution)/shard_map/ppermute | solution.py:18
  82.5 5.0 %collective-permute-start.4 = (bf16[192,3584]{1,0:T(8,128)(2,1)S(1)}, bf16[192,3584]{1,0:T(8,128)(2,1)S(1)}, u32[]{:S(2)}, u32[]{:S(2)}) collective-permute-start(bf16[192,3584]{1,0:T(8,128)(2,1)S(1)} %pad_maximum_fusion.1), channel_id=1, source_target_pairs={{0,32},{32,0},{1,33},{33,1},{2,34},{34,2},{3,35},{35,3},{4,36},{36... | collective-permute-start | bytes 4128776 | tf_op jit(solution)/shard_map/ppermute | solution.py:18
  89.7 5.0 %collective-permute-start.6 = (bf16[192,3584]{1,0:T(8,128)(2,1)S(1)}, bf16[192,3584]{1,0:T(8,128)(2,1)S(1)}, u32[]{:S(2)}, u32[]{:S(2)}) collective-permute-start(bf16[192,3584]{1,0:T(8,128)(2,1)S(1)} %slice.161), channel_id=1, source_target_pairs={{0,32},{32,0},{1,33},{33,1},{2,34},{34,2},{3,35},{35,3},{4,36},{36... | collective-permute-start | bytes 4128776 | tf_op jit(solution)/shard_map/ppermute | solution.py:18
  95.1 25.5 %collective-permute-start.7 = (bf16[64,3584]{1,0:T(8,128)(2,1)S(1)}, bf16[64,3584]{1,0:T(8,128)(2,1)S(1)}, u32[]{:S(2)}, u32[]{:S(2)}) collective-permute-start(bf16[64,3584]{1,0:T(8,128)(2,1)S(1)} %get-tuple-element.22), channel_id=1, source_target_pairs={{0,384},{128,0},{256,128},{384,256},{1,385},{129,1},{257,129},{385... | collective-permute-start | bytes 1376264 | tf_op jit(solution)/shard_map/ppermute | solution.py:13
  100.7 25.2 %collective-permute-start.8 = (bf16[64,3584]{1,0:T(8,128)(2,1)S(1)}, bf16[64,3584]{1,0:T(8,128)(2,1)S(1)}, u32[]{:S(2)}, u32[]{:S(2)}) collective-permute-start(bf16[64,3584]{1,0:T(8,128)(2,1)S(1)} %get-tuple-element.24), channel_id=1, source_target_pairs={{0,128},{128,256},{256,384},{384,0},{1,129},{129,257},{257,385},{3... | collective-permute-start | bytes 1376264 | tf_op jit(solution)/shard_map/ppermute | solution.py:13
  102.6 23.3 %collective-permute-start.9 = (bf16[64,3584]{1,0:T(8,128)(2,1)S(1)}, bf16[64,3584]{1,0:T(8,128)(2,1)S(1)}, u32[]{:S(2)}, u32[]{:S(2)}) collective-permute-start(bf16[64,3584]{1,0:T(8,128)(2,1)S(1)} %get-tuple-element.23), channel_id=1, source_target_pairs={{0,256},{128,384},{256,0},{384,128},{1,257},{129,385},{257,1},{385... | collective-permute-start | bytes 1376264 | tf_op jit(solution)/shard_map/ppermute | solution.py:13
  109.5 23.2 %collective-permute-start.10 = (f32[1]{0:T(128)}, f32[1]{0:T(128)}, u32[]{:S(2)}, u32[]{:S(2)}) collective-permute-start(f32[1]{0:T(128)} %bitcast.36), channel_id=1, source_target_pairs={{0,64},{64,0},{1,65},{65,1},{2,66},{66,2},{3,67},{67,3},{4,68},{68... | collective-permute-start | bytes 20 | tf_op jit(solution)/shard_map/ppermute | solution.py:18
  127.0 11.7 %all-to-all-start.1 = ((bf16[4,64,896]{2,1,0:T(8,128)(2,1)}), bf16[4,64,896]{2,1,0:T(8,128)(2,1)S(1)}, u32[]{:S(2)}, u32[]{:S(2)}) async-start(bf16[4,64,896]{2,1,0:T(8,128)(2,1)} %pad_maximum_fusion.3), calls=%async_computation.1 | async-start | bytes 917504 | tf_op jit(solution)/shard_map/all_to_all | solution.py:131
  139.8 10.3 %collective-permute-start.11 = (f32[1]{0:T(128)}, f32[1]{0:T(128)}, u32[]{:S(2)}, u32[]{:S(2)}) collective-permute-start(f32[1]{0:T(128)} %add.119), channel_id=1, source_target_pairs={{0,32},{32,0},{1,33},{33,1},{2,34},{34,2},{3,35},{35,3},{4,36},{36... | collective-permute-start | bytes 20 | tf_op jit(solution)/shard_map/ppermute | solution.py:18
  143.4 32.1 %all-to-all-start.2 = ((bf16[16,112,96]{1,2,0:T(8,128)(2,1)}), bf16[16,112,96]{1,2,0:T(8,128)(2,1)S(1)}, u32[]{:S(2)}, u32[]{:S(2)}) async-start(bf16[16,112,96]{1,2,0:T(8,128)(2,1)} %copy.123), calls=%async_computation.2 | async-start | bytes 786432 | tf_op jit(solution)/shard_map/all_to_all | solution.py:138
  150.7 5.4 %collective-permute-start.12 = (f32[1]{0:T(128)}, f32[1]{0:T(128)}, u32[]{:S(2)}, u32[]{:S(2)}) collective-permute-start(f32[1]{0:T(128)} %add.120), channel_id=1, source_target_pairs={{0,128},{128,0},{256,384},{384,256},{1,129},{129,1},{257,385},{385... | collective-permute-start | bytes 20 | tf_op jit(solution)/shard_map/ppermute | solution.py:18
  156.8 6.9 %collective-permute-start.13 = (f32[1]{0:T(128)}, f32[1]{0:T(128)}, u32[]{:S(2)}, u32[]{:S(2)}) collective-permute-start(f32[1]{0:T(128)} %add.121), channel_id=1, source_target_pairs={{0,256},{128,384},{256,0},{384,128},{1,257},{129,385},{257,1},{385... | collective-permute-start | bytes 20 | tf_op jit(solution)/shard_map/ppermute | solution.py:18
